TPU v7x, 256 devices: a whole 4x4x8 slice. The times are simulated.
256 devices in a mesh: segment: 4 (over x), ctx: 32 (over y, z), tp: 2 (over core).
Axes of the slice: x: 4, y: 4, z: 8, core: 2. Of those that a mesh axis runs over, the one named last changes fastest.
Arguments:
- mamba_input: bfloat16 [4, 4096, 8192], P('segment', 'ctx', 'tp'), may hold values from -13 to 13
- mamba_gate: bfloat16 [4, 4096, 8192], P('segment', 'ctx', 'tp'), may hold values from -6 to 6
- step_size: bfloat16 [4, 4096, 128], P('segment', 'ctx', 'tp'), may hold values from 0 to 2, as said below
- state_maps: bfloat16 [4, 4096, 256], P('segment', 'ctx'), may hold values from -3 to 3
- decay_rate: float32 [128], P('tp'), may hold values from 0.5 to 2
- skip_gain: float32 [128], P('tp'), may hold values from 0.5 to 1.5
- norm_gain: float32 [8192], P('tp'), may hold values from 0.1 to 1.9
- queries: bfloat16 [4, 4096, 8192], P('segment', 'ctx', 'tp'), may hold values from -155 to 154
- keys: bfloat16 [4, 4096, 1024], P('segment', 'ctx', 'tp'), may hold values from -5 to 5
- values: bfloat16 [4, 4096, 1024], P('segment', 'ctx', 'tp'), may hold values from -6 to 6
- source_len: int32 [4], P('segment'), may hold values from 1638 to 3685
Outputs:
- mamba_handed: bfloat16 [4, 4096, 8192], P('segment', 'ctx', 'tp')
- attention_handed: bfloat16 [4, 4096, 8192], P('segment', 'ctx', 'tp')
Inputs may be any that keep to these rules, and one draw needn't show every extreme that they name: `step_size`: positive.
All inputs are finite; a program needn't handle non-finite values.
Results may differ from a plain program's by a relative error of at most 0.0095.
Values may be sent and summed in bfloat16 or wider, within the bound.
A program may use at most 320 MiB of HBM per device.

v0:
```python
import math

import jax
import jax.numpy as jnp
from jax import lax
from jax.sharding import PartitionSpec as P

QUERY_HEADS = 64
KEY_VALUE_HEADS = 8
HEAD_WIDTH = 128
NST = 128
EM = 8192
HP = 64
BLOCK_LEN = 128


precise = lax.Precision.HIGHEST


def from_behind(array, axis, by):
    size = lax.axis_size(axis)
    return lax.ppermute(array, axis, [(i, (i + by) % size) for i in range(size)])


def join_states(earlier, later):
    return (earlier[0] + later[0], jnp.exp(later[0])[..., None, None] * earlier[1] + later[1])


def scan_blocks(mixer_in, step_in, maps_in, speed_collection, skips):
    tok_rows = mixer_in.shape[0]
    head_count = step_in.shape[1]
    block_len = min(BLOCK_LEN, tok_rows)
    blocks = tok_rows // block_len
    step_float = step_in.astype(jnp.float32).reshape(blocks, block_len, head_count)
    log_decay = -speed_collection[None, None, :] * step_float
    cum_log = jnp.cumsum(log_decay, axis=1)
    x_float = mixer_in.astype(jnp.float32).reshape(blocks, block_len, head_count, HP)
    b_float = maps_in[:, :NST].astype(jnp.float32).reshape(blocks, block_len, NST)
    c_float = maps_in[:, NST:].astype(jnp.float32).reshape(blocks, block_len, NST)
    gram = jnp.einsum("cin,cjn->cij", c_float, b_float, precision=precise)
    lower_tri = (jnp.arange(block_len)[:, None] >= jnp.arange(block_len)[None, :])[None, :, :, None]
    differ = cum_log[:, :, None, :] - cum_log[:, None, :, :]
    decay = jnp.where(lower_tri, jnp.exp(jnp.where(lower_tri, differ, 0.0)), 0.0)
    weights = gram[..., None] * decay * step_float[:, None, :, :]
    inner_out = jnp.einsum("cijh,cjhp->cihp", weights, x_float, precision=precise)
    tail_decay = jnp.exp(cum_log[:, -1:, :] - cum_log) * step_float
    block_states = jnp.einsum("cjh,cjn,cjhp->chnp", tail_decay, b_float, x_float, precision=precise)
    block_logs = cum_log[:, -1, :]
    inc_logs, inc_states = lax.associative_scan(join_states, (block_logs, block_states), axis=0)
    entering = jnp.concatenate([jnp.zeros_like(block_states[:1]), inc_states[:-1]], axis=0)
    enter_logs = jnp.concatenate([jnp.zeros_like(block_logs[:1]), inc_logs[:-1]], axis=0)
    outer_out = jnp.exp(cum_log)[..., None] * jnp.einsum(
        "cin,chnp->cihp", c_float, entering, precision=precise
    )
    mixed = inner_out + outer_out + skips[None, None, :, None] * x_float
    cum_block = (cum_log + enter_logs[:, None, :]).reshape(tok_rows, head_count)
    return (mixed.reshape(tok_rows, head_count, HP), inc_states[-1], inc_logs[-1], cum_block)


def on_device(
    mamba_input,
    mamba_gate,
    step_size,
    state_maps,
    decay_rate,
    skip_gain,
    norm_gain,
    queries,
    keys,
    values,
    source_len,
):
    mixer_in = mamba_input[0]
    gate_in = mamba_gate[0]
    step_in = step_size[0]
    maps_in = state_maps[0]
    tok_rows = mixer_in.shape[0]
    ctx_index = lax.axis_index("ctx")
    chan_rows, chan_steps = (
        lax.all_to_all(mixer_in, "ctx", split_axis=1, concat_axis=0, tiled=True),
        lax.all_to_all(step_in, "ctx", split_axis=1, concat_axis=0, tiled=True),
    )
    all_maps = lax.all_gather(maps_in, "ctx", axis=0, tiled=True)
    sub_heads = chan_steps.shape[1]
    rate_sub = lax.dynamic_slice_in_dim(decay_rate, ctx_index * sub_heads, sub_heads)
    skip_sub = lax.dynamic_slice_in_dim(skip_gain, ctx_index * sub_heads, sub_heads)
    chan_out, _, _, _ = scan_blocks(chan_rows, chan_steps, all_maps, rate_sub, skip_sub)
    chan_out = chan_out.reshape(chan_rows.shape[0], sub_heads * HP).astype(jnp.bfloat16)
    raw = lax.all_to_all(chan_out, "ctx", split_axis=0, concat_axis=1, tiled=True)
    gated = raw.astype(jnp.float32) * jax.nn.silu(gate_in.astype(jnp.float32))
    square_sums = lax.psum(jnp.sum(gated * gated, axis=-1), "tp")
    mean_sq = square_sums / EM
    mamba_out = (gated * lax.rsqrt(mean_sq + 1e-05)[:, None] * norm_gain[None, :]).astype(
        jnp.bfloat16
    )
    query_in = queries[0]
    kv_local = keys.shape[2] // HEAD_WIDTH
    group_width = QUERY_HEADS // KEY_VALUE_HEADS
    query_head_rows = query_in.reshape(tok_rows, kv_local, group_width, HEAD_WIDTH)
    source = source_len[0]
    query_pos = ctx_index * tok_rows + jnp.arange(tok_rows, dtype=jnp.int32)
    scale = 1.0 / math.sqrt(HEAD_WIDTH)
    start_max = jnp.full((kv_local, group_width, tok_rows), -1e30, jnp.float32)
    key_piece = lax.all_gather(keys[0], "ctx", axis=0, tiled=True)
    value_piece = lax.all_gather(values[0], "ctx", axis=0, tiled=True)
    piece_rows = key_piece.shape[0]
    key_head_rows = key_piece.reshape(piece_rows, kv_local, HEAD_WIDTH)
    value_head_rows = value_piece.reshape(piece_rows, kv_local, HEAD_WIDTH)
    key_pos = jnp.arange(piece_rows, dtype=jnp.int32)
    visible = (key_pos[None, :] <= query_pos[:, None]) | (key_pos[None, :] < source)
    scores = (
        jnp.einsum(
            "tkgd,skd->kgts", query_head_rows, key_head_rows, preferred_element_type=jnp.float32
        )
        * scale
    )
    scores = jnp.where(visible[None, None], scores, -jnp.inf)
    new_max = jnp.maximum(start_max, jnp.max(scores, axis=-1))
    weights = jnp.exp(scores - new_max[..., None])
    new_total = jnp.sum(weights, axis=-1)
    product = jnp.einsum(
        "kgts,skd->kgtd",
        weights.astype(jnp.bfloat16),
        value_head_rows,
        preferred_element_type=jnp.float32,
    )
    attention_out = (
        (product / new_total[..., None])
        .transpose(2, 0, 1, 3)
        .reshape(tok_rows, kv_local * group_width * HEAD_WIDTH)
        .astype(jnp.bfloat16)
    )
    mamba_next, attention_next = from_behind((mamba_out, attention_out), "segment", 1)
    return (mamba_next[None], attention_next[None])


def solution(mesh):
    placed = (
        P("segment", "ctx", "tp"),
        P("segment", "ctx", "tp"),
        P("segment", "ctx", "tp"),
        P("segment", "ctx", None),
        P("tp"),
        P("tp"),
        P("tp"),
        P("segment", "ctx", "tp"),
        P("segment", "ctx", "tp"),
        P("segment", "ctx", "tp"),
        P("segment"),
    )
    return jax.shard_map(
        on_device,
        mesh=mesh,
        in_specs=placed,
        out_specs=(P("segment", "ctx", "tp"), P("segment", "ctx", "tp")),
        check_vma=False,
    )
```

profile of v0, /device:TPU:1, one launch (start us, length us, event | category | flops | bytes accessed | tf_op | source)
XLA Modules:
  0.0 348.9 jit_solution(2937649183413915487)
XLA Ops:
  7.9 12.0 %all-to-all-start = ((bf16[128,32,2]{0,2,1:T(2,128)(2,1)}), bf16[128,32,2]{0,2,1:T(2,128)(2,1)S(1)}, u32[]{:S(2)}, u32[]{:S(2)}) async-start(bf16[128,32,2]{0,2,1:T(2,128)(2,1)} %bitcast.126), calls=%async_computation | async-start | bytes 32768 | tf_op jit(solution)/shard_map/all_to_all | solution.py:81
  20.0 1.7 copy.106
  23.0 2.3 copy.117
  25.4 3.2 all-to-all-done
  28.5 6.1 %all-to-all-start.1 = ((bf16[128,32,128]{0,2,1:T(8,128)(2,1)}), bf16[128,32,128]{0,2,1:T(8,128)(2,1)S(1)}, u32[]{:S(2)}, u32[]{:S(2)}) async-start(bf16[128,32,128]{0,2,1:T(8,128)(2,1)} %bitcast.5), calls=%async_computation.1 | async-start | bytes 2097152 | tf_op jit(solution)/shard_map/all_to_all | solution.py:80
  34.7 2.8 copy.87
  37.5 1.8 fusion.61
  40.2 1.3 copy.94
  42.0 1.9 copy.88
  43.9 1.6 exp.51
  47.4 3.3 copy.92
  51.0 40.0 %all-gather.7.cloned.1.call-done = bf16[1,4096,256]{2,1,0:T(8,128)(2,1)} async-done(((bf16[1,128,256]{2,1,0:T(8,128)(2,1)}), bf16[1,4096,256]{2,1,0:T(8,128)(2,1)}) %all-gather.7.cloned.1.call-update) | async-done | bytes 2097168 | tf_op jit(solution)/shard_map/all_gather | solution.py:83
  91.0 3.0 fusion.54
  94.0 2.4 fusion.36
  100.6 1.6 pad.34
  102.2 1.5 pad_add_fusion
  103.7 3.4 pad.35
  107.1 1.7 add.123
  108.8 5.1 %pad.37 = f32[8,2,128,64]{2,3,1,0:T(8,128)} pad(f32[4,2,128,64]{2,3,1,0:T(8,128)} %add.123, f32[]{:T(128)} %constant.9.clone.1), padding=1_0_1x0_0_0x0_0_0x0_0_0 | pad | bytes 786436 | tf_op jit(solution)/shard_map/pad | solution.py:49
  115.0 3.2 pad.36
  118.3 2.1 add.125
  120.4 1.4 fusion.45
  122.6 9.2 %pad.38 = f32[16,2,128,64]{2,3,1,0:T(8,128)} pad(f32[8,2,128,64]{2,3,1,0:T(8,128)} %pad_maximum_fusion.1, f32[]{:T(128)} %constant.9.clone.1), padding=0_1_1x0_0_0x0_0_0x0_0_0 | pad | bytes 1572868 | tf_op jit(solution)/shard_map/pad | solution.py:49
  131.8 9.2 %pad.39 = f32[16,2,128,64]{2,3,1,0:T(8,128)} pad(f32[8,2,128,64]{2,3,1,0:T(8,128)} %add.125, f32[]{:T(128)} %constant.9.clone.1), padding=1_0_1x0_0_0x0_0_0x0_0_0 | pad | bytes 1572868 | tf_op jit(solution)/shard_map/pad | solution.py:49
  141.0 2.7 add.127
  143.7 16.6 %pad.73 = f32[32,2,128,64]{2,3,1,0:T(8,128)} pad(f32[16,2,128,64]{2,3,1,0:T(8,128)} %add.127, f32[]{:T(128)} %constant.9.clone.1), padding=1_0_1x0_0_0x0_0_0x0_0_0 | pad | bytes 3145732
  160.2 1.7 fusion.44
  163.0 12.4 %pad.51 = f32[31,2,128,64]{2,3,1,0:T(8,128)S(1)} pad(f32[16,2,128,64]{2,3,1,0:T(8,128)} %pad_maximum_fusion, f32[]{:T(128)} %constant.9.clone.1), padding=0_0_1x0_0_0x0_0_0x0_0_0 | pad | bytes 3080196 | tf_op jit(solution)/shard_map/slice | solution.py:50
  175.4 2.4 fusion.62
  177.9 4.9 %fusion.6 = f32[32,2,128,64]{2,3,1,0:T(8,128)S(1)} fusion(bf16[32,128,2,64]{1,3,2,0:T(8,128)(2,1)S(1)} %bitcast.106, f32[32,128,2]{1,2,0:T(2,128)S(1)} %copy-done.9, f32[32,128,2]{1,2,0:T(2,128)S(1)} %copy-done.8, f32[32,128,128]{2,1,0:T(8,128)S(1)} %fusion.62, pred[128,128]{1,0:T(8,128)(4,1)S(1)} %copy-done.11), kind=kOutput, calls=%fused_computation.7 | convolution fusion | flops 810549248 | bytes 5324800 | tf_op jit(solution)/shard_map/cijh,cjhp->cihp/dot_general | solution.py:45
  182.9 3.3 fusion.15
  186.2 5.2 %all-to-all-start.2 = ((bf16[32,128,128]{1,2,0:T(8,128)(2,1)}), bf16[32,128,128]{1,2,0:T(8,128)(2,1)S(1)}, u32[]{:S(2)}, u32[]{:S(2)}) async-start(bf16[32,128,128]{1,2,0:T(8,128)(2,1)} %bitcast.115), calls=%async_computation.2 | async-start | bytes 2097152 | tf_op jit(solution)/shard_map/all_to_all | solution.py:89
  192.1 1.6 copy.121
  194.4 1.4 copy.122
  195.8 2.1 fusion.32
  198.0 12.7 %all-to-all-done.2 = bf16[32,128,128]{1,2,0:T(8,128)(2,1)S(1)} async-done(((bf16[32,128,128]{1,2,0:T(8,128)(2,1)}), bf16[32,128,128]{1,2,0:T(8,128)(2,1)S(1)}, u32[]{:S(2)}, u32[]{:S(2)}) %all-to-all-start.2) | async-done | bytes 1048608 | tf_op jit(solution)/shard_map/all_to_all | solution.py:89
  210.7 1.6 convert_element_type.78
  212.3 2.9 copy.118
  215.2 2.3 fusion.24
  217.6 12.2 %psum.7 = f32[128]{0:T(128)S(1)} all-reduce(f32[128]{0:T(128)S(1)} %fusion.24), channel_id=1, replica_groups=mesh['segment'=4,'ctx'=32,'tp'=2] {'tp'}, use_global_device_ids=true, to_apply=%region_2.3 | all-reduce | flops 128 | bytes 1024 | tf_op jit(solution)/shard_map/psum | solution.py:91
  229.7 2.6 fusion.31
  233.6 26.5 %fusion.2 = (f32[4,8,128]{2,1,0:T(8,128)S(1)}, f32[4,4096,128,8]{2,1,3,0:T(8,128)}) fusion(pred[128,4096]{0,1:T(8,128)(4,1)S(1)} %fusion.32, bf16[4096,4,128,1]{0,2,3,1:T(8,128)(2,1)} %bitcast.116, bf16[128,4,8,128]{3,2,1,0:T(8,128)(2,1)S(1)} %bitcast.114), kind=kOutput, calls=%fused_computation.4 | convolution fusion | flops 4345294848 | bytes 72892416 | tf_op jit(solution)/shard_map/tkgd,skd->kgts/dot_general | solution.py:112
  260.0 21.9 %fusion = f32[4,8,128]{2,1,0:T(8,128)S(1)} fusion(f32[4,4096,128,8]{2,1,3,0:T(8,128)} %get-tuple-element.17, f32[4,8,128]{2,1,0:T(8,128)S(1)} %broadcast_maximum_fusion, pred[128,4096]{0,1:T(8,128)(4,1)S(1)} %fusion.32), kind=kLoop, calls=%fused_computation.2 | loop fusion | flops 67104768 | bytes 67665920 | tf_op jit(solution)/shard_map/reduce_sum | solution.py:120
  282.0 6.4 %copy.109 = bf16[1,4096,512]{1,2,0:T(8,128)(2,1)} copy(bf16[1,4096,512]{2,1,0:T(8,128)(2,1)} %all-gather.11.cloned.1.call-done) | data formatting | bytes 8388608 | tf_op jit(solution)/shard_map/all_gather | solution.py:105
  288.3 25.5 %fusion.16 = bf16[128,4,8,128]{0,3,2,1:T(8,128)(2,1)S(1)} fusion(bf16[4096,4,128,1]{0,2,3,1:T(8,128)(2,1)} %bitcast.117, f32[4,4096,128,8]{2,1,3,0:T(8,128)} %get-tuple-element.17, f32[4,8,128]{2,1,0:T(8,128)S(1)} %broadcast_maximum_fusion, pred[128,4096]{0,1:T(8,128)(4,1)S(1)} %fusion.32, f32[128,4,8]{0,2,1:T(8,128)S(1)} %bitcast.127), kind=kOutput, calls=%fused_computation.20 | convolution fusion | flops 4363124736 | bytes 72908800 | tf_op jit(solution)/shard_map/kgts,skd->kgtd/dot_general | solution.py:121
  314.4 1.3 collective-permute-start.1
  315.6 23.5 %collective-permute-done.1 = bf16[128,4096]{1,0:T(8,128)(2,1)S(1)} collective-permute-done((bf16[128,4096]{1,0:T(8,128)(2,1)S(1)}, bf16[128,4096]{1,0:T(8,128)(2,1)S(1)}, u32[]{:S(2)}, u32[]{:S(2)}) %collective-permute-start.1) | collective-permute-done | bytes 1048608 | tf_op jit(solution)/shard_map/ppermute | solution.py:22
  339.1 2.3 copy.133
  (96 shorter events, 16.7 us)
Async XLA Ops:
  7.2 18.1 %copy-start.12 = (f32[64]{0:T(128)S(1)}, f32[64]{0:T(128)}, u32[]{:S(2)}) copy-start(f32[64]{0:T(128)} %param.16) | copy-start | bytes 772
  7.2 83.8 %all-gather.7.cloned.1.call-start = ((), (), s32[]{:S(2)}) async-start(), calls=%async_computation.3 | async-start | bytes 2162688 | tf_op jit(solution)/shard_map/all_gather | solution.py:83
  7.9 20.6 %all-to-all-start = ((bf16[128,32,2]{0,2,1:T(2,128)(2,1)}), bf16[128,32,2]{0,2,1:T(2,128)(2,1)S(1)}, u32[]{:S(2)}, u32[]{:S(2)}) async-start(bf16[128,32,2]{0,2,1:T(2,128)(2,1)} %bitcast.126), calls=%async_computation | async-start | bytes 32768 | tf_op jit(solution)/shard_map/all_to_all | solution.py:81
  20.0 213.6 %all-gather.9.cloned.1.call-start = ((), (), s32[]{:S(2)}) async-start(), calls=%async_computation.4 | async-start | bytes 4325376 | tf_op jit(solution)/shard_map/all_gather | solution.py:104
  28.5 65.4 %all-to-all-start.1 = ((bf16[128,32,128]{0,2,1:T(8,128)(2,1)}), bf16[128,32,128]{0,2,1:T(8,128)(2,1)S(1)}, u32[]{:S(2)}, u32[]{:S(2)}) async-start(bf16[128,32,128]{0,2,1:T(8,128)(2,1)} %bitcast.5), calls=%async_computation.1 | async-start | bytes 2097152 | tf_op jit(solution)/shard_map/all_to_all | solution.py:80
  97.2 1.0 copy-start.2
  98.3 0.8 copy-start.4
  99.3 0.6 copy-start.5
  99.3 15.7 %slice-start.1 = ((f32[8,2,128,64]{2,3,1,0:T(8,128)}), f32[1,2,128,64]{2,3,1,0:T(8,128)S(1)}, s32[]{:S(2)}) async-start(f32[8,2,128,64]{2,3,1,0:T(8,128)} %copy-done.4), calls=%async_computation.7 | async-start | bytes 131072 | tf_op jit(solution)/shard_map/slice | solution.py:49
  115.0 6.7 %slice-start = ((f32[16,2,128,64]{2,3,1,0:T(8,128)}), f32[1,2,128,64]{2,3,1,0:T(8,128)S(1)}, s32[]{:S(2)}) async-start(f32[16,2,128,64]{2,3,1,0:T(8,128)} %copy-done.2), calls=%async_computation.6 | async-start | bytes 131072 | tf_op jit(solution)/shard_map/slice | solution.py:49
  160.2 1.8 copy-start.6
  175.4 2.4 copy-start.8
  175.4 2.4 copy-start.9
  175.4 2.4 copy-start.11
  177.9 5.0 %copy-start = (f32[32,2,128,64]{2,3,1,0:T(8,128)S(1)}, f32[32,2,128,64]{2,3,1,0:T(8,128)}, u32[]{:S(2)}) copy-start(f32[32,2,128,64]{2,3,1,0:T(8,128)} %pad.73) | copy-start | bytes 6291460
  177.9 5.0 %copy-start.1 = (bf16[4096,128]{1,0:T(8,128)(2,1)S(1)}, bf16[4096,128]{1,0:T(8,128)(2,1)}, u32[]{:S(2)}) copy-start(bf16[4096,128]{1,0:T(8,128)(2,1)} %get-tuple-element.3) | copy-start | bytes 3145732
  177.9 5.0 %copy-start.7 = (f32[32,128,2]{1,2,0:T(2,128)S(1)}, f32[32,128,2]{1,2,0:T(2,128)}, u32[]{:S(2)}) copy-start(f32[32,128,2]{1,2,0:T(2,128)} %copy.92) | copy-start | bytes 98308
  186.2 5.9 %copy-start.3 = (bf16[1,128,4096]{2,1,0:T(8,128)(2,1)S(1)}, bf16[1,128,4096]{2,1,0:T(8,128)(2,1)}, u32[]{:S(2)}) copy-start(bf16[1,128,4096]{2,1,0:T(8,128)(2,1)} %param.12) | copy-start | bytes 3145732
  186.2 24.5 %all-to-all-start.2 = ((bf16[32,128,128]{1,2,0:T(8,128)(2,1)}), bf16[32,128,128]{1,2,0:T(8,128)(2,1)S(1)}, u32[]{:S(2)}, u32[]{:S(2)}) async-start(bf16[32,128,128]{1,2,0:T(8,128)(2,1)} %bitcast.115), calls=%async_computation.2 | async-start | bytes 2097152 | tf_op jit(solution)/shard_map/all_to_all | solution.py:89
  191.3 90.6 %all-gather.11.cloned.1.call-start = ((), (), s32[]{:S(2)}) async-start(), calls=%async_computation.5 | async-start | bytes 4325376 | tf_op jit(solution)/shard_map/all_gather | solution.py:105
  215.2 14.5 %copy-start.10 = (f32[4096]{0:T(1024)S(1)}, f32[4096]{0:T(1024)}, u32[]{:S(2)}) copy-start(f32[4096]{0:T(1024)} %param.17) | copy-start | bytes 49156
  232.3 83.3 %collective-permute-start = (bf16[128,4096]{1,0:T(8,128)(2,1)S(1)}, bf16[128,4096]{1,0:T(8,128)(2,1)}, u32[]{:S(2)}, u32[]{:S(2)}) collective-permute-start(bf16[128,4096]{1,0:T(8,128)(2,1)S(1)} %fusion.31), channel_id=1, source_target_pairs={{0,64},{64,128},{128,192},{192,0},{1,65},{65,129},{129,193},{193,1... | collective-permute-start | bytes 3145736 | tf_op jit(solution)/shard_map/ppermute | solution.py:22
  314.4 24.7 %collective-permute-start.1 = (bf16[128,4096]{1,0:T(8,128)(2,1)S(1)}, bf16[128,4096]{1,0:T(8,128)(2,1)S(1)}, u32[]{:S(2)}, u32[]{:S(2)}) collective-permute-start(bf16[128,4096]{1,0:T(8,128)(2,1)S(1)} %copy.111), channel_id=1, source_target_pairs={{0,64},{64,128},{128,192},{192,0},{1,65},{65,129},{129,193},{193,1... | collective-permute-start | bytes 3145736 | tf_op jit(solution)/shard_map/ppermute | solution.py:22
Sparse Core Ops, SparseCore 0:
  10.6 80.3 all-gather.6
  93.4 81.0 all-gather.8
  194.7 85.0 all-gather.10
where the time goes:
time: 356 us; the launch traced here: 349 us
  local copies, waits for them, and re-layouts  101 us (28%)
  waiting for transfers between devices  80.7 us (23%)
  matrix products  64.9 us (18%)
  other arithmetic  49.3 us (14%)
  starting transfers between devices  25.9 us (7%)
  between operations  14.7 us (4%)
  blocking collectives  12.2 us (3%)
    all_gather x1, waiting for transfers between devices, on_device(): all_maps = lax.all_gather(maps_in, 'ctx', axis=0, tiled=True)  40 us
    pad x6, local copies, waits for them, and re-layouts, scan_blocks(): lax.associative_scan(join_states, (block_logs, block_states), axis=0)  31.7 us
    dot_general x1, matrix products, on_device(): jnp.einsum('tkgd,skd->kgts', query_head_rows, key_head_rows, preferred_el...  26.5 us
    dot_general x1, matrix products, on_device(): jnp.einsum('kgts,skd->kgtd', weights.astype(jnp.bfloat16), value_head_row...  25.5 us
    unnamed x31, local copies, waits for them, and re-layouts  25.3 us
    ppermute x2, waiting for transfers between devices, from_behind(): lax.ppermute(array, axis, [(i, (i + by) % size) for i in range(size)])  23.5 us
    reduce_sum x1, other arithmetic, on_device(): new_total = jnp.sum(weights, axis=-1)  21.9 us
    all_to_all x1, waiting for transfers between devices, on_device(): lax.all_to_all(chan_out, 'ctx', split_axis=0, concat_axis=1, tiled=True)  12.7 us
  transfers between devices with their start and end apart: 8, of which 4 were waited for; matrix products, arithmetic and copies ran while one was open for 60% of the time, Pallas kernels for 0%

commit v1 on v0

v1 whole, which is shorter than its diff:
```python
import functools
import math

import jax
import jax.numpy as jnp
from jax import lax
from jax.experimental import pallas as pl
from jax.experimental.pallas import tpu as pltpu
from jax.sharding import PartitionSpec as P

QUERY_HEADS = 64
KEY_VALUE_HEADS = 8
GROUP = QUERY_HEADS // KEY_VALUE_HEADS
D = 128
NST = 128
HP = 64
Z_RING = 8
MESH = pl.DeviceIdType.MESH
NEG = -1e30
HIGH = lax.Precision.HIGHEST
F32 = jnp.float32
BF16 = jnp.bfloat16


def nt_dot(a, b):
    return lax.dot_general(a, b, (((1,), (1,)), ((), ())), preferred_element_type=F32)


def section_kernel(
    dims,
    x_ref, gate_ref, step_ref, maps_ref, rate_ref, skip_ref, gain_ref, q_ref, k_ref, v_ref, src_ref,
    mo_ref, ao_ref,
    kv, qb, sb, inbox, so, sin, yb, cum_e, ecum_e, tail_e, cum_t, dt_t, gram,
    sc, lim, mx, ls, acc, ob, mob, sqs, sqr,
    yk_send, yk_recv, q_send, q_recv, loc, ring_send, ring_recv, s_send, s_recv, r_send, r_recv,
    ao_send, ao_recv, mo_send, mo_recv, sq_send, sq_recv,
):
    nx, ny, nz, T, em = dims
    nc = ny * nz
    seg = lax.axis_index("segment")
    me = lax.axis_index("ctx")
    tp = lax.axis_index("tp")
    y = me // nz
    z = lax.rem(me, nz)
    after = lax.rem(seg + 1, nx)
    before = lax.rem(seg + nx - 1, nx)
    half = nz // 2

    def remote(src, dst, ssem, rsem, dev):
        return pltpu.make_async_remote_copy(
            src_ref=src, dst_ref=dst, send_sem=ssem, recv_sem=rsem, device_id=dev, device_id_type=MESH
        )

    def at_ctx(c):
        return (seg, c, tp)

    barrier = pltpu.get_barrier_semaphore()

    @pl.loop(1, nc)
    def _(i):
        pl.semaphore_signal(barrier, inc=1, device_id=at_ctx(lax.rem(me + i, nc)), device_id_type=MESH)

    for i in range(ny):
        pl.semaphore_signal(barrier, inc=1, device_id=(before, i * nz + z, tp), device_id_type=MESH)
    pl.semaphore_signal(barrier, inc=1, device_id=(seg, me, 1 - tp), device_id_type=MESH)
    pl.semaphore_wait(barrier, nc - 1 + ny + 1)

    def col(i, w):
        return pl.ds(pl.multiple_of(i * w, w), w)

    def yk_copy(i, kvi, src):
        o = lax.rem(y + i, ny)
        return remote(
            src.at[:, col(o, D)], kv.at[z, kvi, pl.ds(pl.multiple_of(y * T, T), T)],
            yk_send.at[i, kvi], yk_recv.at[i, kvi], at_ctx(o * nz + z),
        )

    def q_copy(i):
        o = lax.rem(y + i, ny)
        return remote(
            q_ref.at[:, col(o, GROUP * D)], qb.at[y], q_send.at[i], q_recv.at[i], at_ctx(o * nz + z)
        )

    for i in range(1, ny):
        yk_copy(i, 0, k_ref).start()
        yk_copy(i, 1, v_ref).start()
    own = [
        pltpu.make_async_copy(k_ref.at[:, col(y, D)], kv.at[z, 0, pl.ds(pl.multiple_of(y * T, T), T)], loc.at[0]),
        pltpu.make_async_copy(v_ref.at[:, col(y, D)], kv.at[z, 1, pl.ds(pl.multiple_of(y * T, T), T)], loc.at[1]),
        pltpu.make_async_copy(q_ref.at[:, col(y, GROUP * D)], qb.at[y], loc.at[2]),
    ]
    for c in own:
        c.start()

    heads = em // HP
    row = lax.broadcasted_iota(jnp.int32, (T, T), 0)
    lane = lax.broadcasted_iota(jnp.int32, (T, T), 1)
    low = (row >= lane)
    dt = step_ref[...].astype(F32)
    logs = -rate_ref[...] * dt
    cum = jnp.dot(low.astype(F32), logs, precision=HIGH, preferred_element_type=F32)
    last = cum[T - 1:T, :]
    tail = jnp.exp(last - cum) * dt
    ecum = jnp.exp(cum)
    cum_t[...] = cum.T
    dt_t[...] = dt.T
    width = min(512, em)
    for j in range(em // width):
        hrow = lax.broadcasted_iota(jnp.int32, (heads, width), 0)
        hcol = lax.broadcasted_iota(jnp.int32, (heads, width), 1)
        pick = (hrow == (hcol + j * width) // HP).astype(F32)
        sl = slice(j * width, (j + 1) * width)
        tail_e[:, sl] = jnp.dot(tail, pick, precision=HIGH, preferred_element_type=F32)
        cum_e[:, sl] = jnp.dot(cum, pick, precision=HIGH, preferred_element_type=F32)
        ecum_e[:, sl] = jnp.dot(ecum, pick, precision=HIGH, preferred_element_type=F32)

    right = at_ctx(y * nz + lax.rem(z + 1, nz))
    left = at_ctx(y * nz + lax.rem(z + nz - 1, nz))

    def ring_copy(b, kvi, way):
        return remote(
            kv.at[b, kvi], kv.at[b, kvi], ring_send.at[way, b, kvi], ring_recv.at[b, kvi],
            right if way == 0 else left,
        )

    reach = [[half, half - 1], [half - 1, half]]

    def ring_step(s):
        for kvi in range(2):
            for way in range(2):
                b = lax.rem(z + nz - s, nz) if way == 0 else lax.rem(z + s, nz)
                if 0 < s <= reach[way][kvi]:
                    ring_copy(b, kvi, way).wait_recv()
                if s < reach[way][kvi]:
                    ring_copy(b, kvi, way).start()

    for i in range(1, ny):
        yk_copy(i, 0, k_ref).wait_recv()
        yk_copy(i, 1, v_ref).wait_recv()
    own[0].wait()
    own[1].wait()
    ring_step(0)

    b_mat = maps_ref[:, :NST]
    c_mat = maps_ref[:, NST:]
    gram[...] = jnp.where(low, nt_dot(c_mat, b_mat), 0.0)
    b_t = b_mat.astype(F32).T.astype(BF16)
    sub16 = lax.broadcasted_iota(jnp.int32, (16, D), 0)

    def state_copy(i, p):
        return remote(sb.at[p], inbox.at[me], s_send.at[i], s_recv.at[me], at_ctx(p))

    def state_of(p):
        scaled = (x_ref[:, col(p, 128)].astype(F32) * tail_e[:, col(p, 128)]).astype(BF16)
        chunk = jnp.dot(b_t, scaled, preferred_element_type=F32)
        decay = ecum_e[T - 1:T, col(p, 128)]
        high = decay.astype(BF16).astype(F32)
        rest = jnp.where(sub16 < 8, high, decay - high)
        return chunk.astype(BF16), rest.astype(BF16)

    @pl.loop(1, nc)
    def _(i):
        p = lax.rem(me + i, nc)
        chunk, rest = state_of(p)
        sb[p, 0:NST] = chunk
        sb[p, NST:NST + 16] = rest
        state_copy(i, p).start()

    chunk, rest = state_of(me)
    inbox[me, 0:NST] = chunk
    inbox[me, NST:NST + 16] = rest

    for i in range(1, ny):
        q_copy(i).start()
    ring_step(1)

    def inner(p):
        xt = x_ref[:, col(p, 128)]
        ce = cum_e[:, col(p, 128)]
        g = gram[...]
        outs = []
        for k in range(2):
            diff = ce[:, k * HP:k * HP + 1] - cum_t[pl.ds(2 * p + k, 1), :]
            w = g * jnp.exp(jnp.minimum(diff, 0.0)) * dt_t[pl.ds(2 * p + k, 1), :]
            outs.append(jnp.dot(w.astype(BF16), xt, preferred_element_type=F32))
        mixed = jnp.where(lane < HP, outs[0], outs[1])
        yb[:, col(p, 128)] = mixed + skip_ref[:, col(p, 128)] * xt.astype(F32)

    parts = max(1, half - 1)
    for s in range(parts):
        @pl.loop(s * nc // parts, (s + 1) * nc // parts)
        def _(p):
            inner(p)
        ring_step(s + 2)

    def back_copy(c):
        return remote(so.at[c], sin.at[me], r_send.at[c], r_recv.at[me], at_ctx(c))

    def wait_state(c):
        remote(sb.at[0], inbox.at[c], s_send.at[0], s_recv.at[c], at_ctx(c)).wait_recv()

    def scan_step(c, carry):
        @pl.when(c != me)
        def _():
            wait_state(c)
        so[c] = carry.astype(BF16)

        @pl.when(c != me)
        def _():
            back_copy(c).start()
        @pl.when(c == me)
        def _():
            sin[me] = carry.astype(BF16)
        rest = inbox[c, NST:NST + 16].astype(F32)
        return carry * (rest[0:1] + rest[8:9]) + inbox[c, 0:NST].astype(F32)

    lax.fori_loop(0, nc, scan_step, jnp.zeros((NST, 128), F32))

    own[2].wait()
    for i in range(1, ny):
        q_copy(i).wait_recv()
    source = src_ref[0]
    scale2 = 1.0 / math.sqrt(D) * math.log2(math.e)
    R = 2 * T
    tiles = GROUP // 2
    keys = ny * T
    lane_k = lax.broadcasted_iota(jnp.int32, (R, T), 1)

    def out_copy(c):
        return remote(
            ob.at[c], ao_ref.at[:, col(y, GROUP * D)], ao_send.at[c], ao_recv.at[y],
            (after, c * nz + z, tp),
        )

    def attend(c):
        pos = c * (nz * T) + z * T + lax.rem(lax.broadcasted_iota(jnp.int32, (R, T), 0), T)
        lim[...] = jnp.maximum(pos + 1, source)
        for t in range(tiles):
            cols = [slice((2 * t + k) * D, (2 * t + k + 1) * D) for k in range(2)]
            q = jnp.concatenate([qb[c, :, cols[0]], qb[c, :, cols[1]]], axis=0)
            mx[...] = jnp.full((R, T), NEG, F32)

            @pl.loop(0, nz)
            def _(b):
                s = nt_dot(q, kv[b, 0])
                top = mx[...]
                for j in range(ny):
                    part = s[:, j * T:(j + 1) * T]
                    if j > 0:
                        part = jnp.where(lane_k + (j * nz * T + b * T) < lim[...], part, NEG)
                    sc[b, :, j * T:(j + 1) * T] = part
                    top = jnp.maximum(top, part)
                mx[...] = top

            m = jnp.max(mx[...], axis=-1, keepdims=True)
            acc[...] = jnp.zeros((R, D), F32)
            ls[...] = jnp.zeros((R, T), F32)

            @pl.loop(0, nz)
            def _(b):
                w = jnp.exp2((sc[b] - m) * scale2)
                total = ls[...]
                for j in range(ny):
                    total = total + w[:, j * T:(j + 1) * T]
                ls[...] = total
                acc[...] += jnp.dot(w.astype(BF16), kv[b, 1], preferred_element_type=F32)

            den = jnp.sum(ls[...], axis=-1, keepdims=True)
            o = (acc[...] / den).astype(BF16)
            ob[c, :, cols[0]] = o[:T]
            ob[c, :, cols[1]] = o[T:]
        out_copy(c).start()

    def sq_copy():
        return remote(sqs, sqr, sq_send, sq_recv, (seg, me, 1 - tp))

    mcols = min(1024, em)

    def mo_copy(j):
        return remote(
            mob.at[:, col(j, mcols)], mo_ref.at[:, col(j, mcols)], mo_send.at[j], mo_recv.at[j], (after, me, tp)
        )

    def finish():
        def step(p, sq):
            @pl.when(p != me)
            def _():
                remote(so.at[0], sin.at[p], r_send.at[0], r_recv.at[p], at_ctx(p)).wait_recv()
            entered = jnp.dot(c_mat, sin[p], preferred_element_type=F32)
            raw = (yb[:, col(p, 128)] + ecum_e[:, col(p, 128)] * entered).astype(BF16).astype(F32)
            g = gate_ref[:, col(p, 128)].astype(F32)
            gated = raw * (g / (1.0 + jnp.exp(-g)))
            yb[:, col(p, 128)] = gated
            return sq + gated * gated
        sqs[...] = lax.fori_loop(0, nc, step, jnp.zeros((T, 128), F32))
        sq_copy().start()
        sq_copy().wait_recv()
        total = jnp.sum(sqs[...] + sqr[...], axis=-1, keepdims=True)
        factor = lax.rsqrt(total / (2 * em) + 1e-5)
        for j in range(em // mcols):
            @pl.loop(0, mcols // 128)
            def _(i):
                p = j * (mcols // 128) + i
                mob[:, col(p, 128)] = (yb[:, col(p, 128)] * factor * gain_ref[:, col(p, 128)]).astype(BF16)
            mo_copy(j).start()

    early = ny - 1
    @pl.loop(0, early)
    def _(c):
        attend(c)
    finish()
    @pl.loop(early, ny)
    def _(c):
        attend(c)

    for i in range(1, ny):
        yk_copy(i, 0, k_ref).wait_send()
        yk_copy(i, 1, v_ref).wait_send()
        q_copy(i).wait_send()
    for s in range(half):
        for kvi in range(2):
            for way in range(2):
                b = lax.rem(z + nz - s, nz) if way == 0 else lax.rem(z + s, nz)
                if s < reach[way][kvi]:
                    ring_copy(b, kvi, way).wait_send()

    @pl.loop(1, nc)
    def _(i):
        p = lax.rem(me + i, nc)
        state_copy(i, p).wait_send()
        back_copy(p).wait_send()

    sq_copy().wait_send()
    for c in range(ny):
        out_copy(c).wait_send()
    for j in range(em // mcols):
        mo_copy(j).wait_send()
        mo_copy(j).wait_recv()
    for c in range(ny):
        remote(ob.at[0], ao_ref.at[:, col(c, GROUP * D)], ao_send.at[0], ao_recv.at[c], (after, me, tp)).wait_recv()


def on_device(mamba_input, mamba_gate, step_size, state_maps, decay_rate, skip_gain, norm_gain,
              queries, keys, values, source_len, *, dims):
    nx, ny, nz, T, em = dims
    nc = ny * nz
    vmem = pl.BlockSpec(memory_space=pltpu.VMEM)
    R = 2 * T
    DMA = pltpu.SemaphoreType.DMA
    out = jax.ShapeDtypeStruct((T, em), BF16)
    mo, ao = pl.pallas_call(
        functools.partial(section_kernel, dims),
        out_shape=(out, jax.ShapeDtypeStruct((T, ny * GROUP * D), BF16)),
        in_specs=[vmem] * 10 + [pl.BlockSpec(memory_space=pltpu.SMEM)],
        out_specs=(pl.BlockSpec(memory_space=pl.ANY), pl.BlockSpec(memory_space=pl.ANY)),
        scratch_shapes=[
            pltpu.VMEM((nz, 2, ny * T, D), BF16),
            pltpu.VMEM((ny, T, GROUP * D), BF16),
            pltpu.VMEM((nc, NST + 16, 128), BF16),
            pltpu.VMEM((nc, NST + 16, 128), BF16),
            pltpu.VMEM((nc, NST, 128), BF16),
            pltpu.VMEM((nc, NST, 128), BF16),
            pltpu.VMEM((T, em), F32),
            pltpu.VMEM((T, em), F32),
            pltpu.VMEM((T, em), F32),
            pltpu.VMEM((T, em), F32),
            pltpu.VMEM((em // HP, T), F32),
            pltpu.VMEM((em // HP, T), F32),
            pltpu.VMEM((T, T), F32),
            pltpu.VMEM((nz, R, ny * T), F32),
            pltpu.VMEM((R, T), jnp.int32),
            pltpu.VMEM((R, T), F32),
            pltpu.VMEM((R, T), F32),
            pltpu.VMEM((R, D), F32),
            pltpu.VMEM((ny, T, GROUP * D), BF16),
            pltpu.VMEM((T, em), BF16),
            pltpu.VMEM((T, 128), F32),
            pltpu.VMEM((T, 128), F32),
            DMA((ny, 2)), DMA((ny, 2)), DMA((ny,)), DMA((ny,)), DMA((3,)),
            DMA((2, nz, 2)), DMA((nz, 2)), DMA((nc,)), DMA((nc,)), DMA((nc,)), DMA((nc,)),
            DMA((ny,)), DMA((ny,)), DMA((max(1, em // 1024),)), DMA((max(1, em // 1024),)),
            DMA(()), DMA(()),
        ],
        compiler_params=pltpu.CompilerParams(
            collective_id=0, has_side_effects=True, vmem_limit_bytes=56 << 20
        ),
    )(
        mamba_input[0], mamba_gate[0], step_size[0], state_maps[0],
        decay_rate[None, :], jnp.repeat(skip_gain, HP)[None, :], norm_gain[None, :],
        queries[0], keys[0], values[0], source_len,
    )
    return mo[None], ao[None]


def solution(mesh):
    nx, nc = mesh.shape["segment"], mesh.shape["ctx"]
    nz = min(Z_RING, nc)
    placed = (
        P("segment", "ctx", "tp"), P("segment", "ctx", "tp"), P("segment", "ctx", "tp"),
        P("segment", "ctx", None), P("tp"), P("tp"), P("tp"),
        P("segment", "ctx", "tp"), P("segment", "ctx", "tp"), P("segment", "ctx", "tp"), P("segment"),
    )
    dims = (nx, nc // nz, nz, 128, 128 * nc)
    return jax.shard_map(
        functools.partial(on_device, dims=dims),
        mesh=mesh,
        in_specs=placed,
        out_specs=(P("segment", "ctx", "tp"), P("segment", "ctx", "tp")),
        check_vma=False,
    )
```

time: 356 us -> 169 us (0.47)
  the two profiles are of different devices: /device:TPU:1 before, /device:TPU:121 now
where the time goes in v1:
time: 169 us
  Pallas kernels  162 us (96%)
  local copies, waits for them, and re-layouts  5.55 us (3%)
    pallas_call x1, Pallas kernels, on_device(): pl.pallas_call(functools.partial(section_kernel, dims), out_shape=(out, j...  162 us
    unnamed x9, local copies, waits for them, and re-layouts  4.78 us

profile of v1, /device:TPU:121, one launch (start us, length us, event | category | flops | bytes accessed | tf_op | source)
XLA Modules:
  0.0 169.2 jit_solution(3088607671355961171)
XLA Ops:
  0.6 0.0 copy-start.1
  1.3 0.0 copy-done.1
  1.3 0.7 copy.13
  2.1 0.0 copy-start.2
  2.1 0.7 copy-done.2
  2.7 0.1 broadcast_in_dim.16
  2.8 0.7 broadcast_in_dim_reshape.3.skip_ref
  3.5 162.4 %shard_map.122 = (bf16[128,4096]{1,0:T(8,128)(2,1)}, bf16[128,4096]{1,0:T(8,128)(2,1)}) custom-call(bf16[128,4096]{1,0:T(8,128)(2,1)} %bitcast.13, bf16[128,4096]{1,0:T(8,128)(2,1)} %bitcast.14, bf16[128,64]{1,0:T(8,128)(2,1)} %bitcast.18, bf16[128,256]{1,0:T(8,128)(2,1)} %bitcast.19, f32[1,64]{1,0:T(1,128)} %bitcast.21, ...), custom_call_target="tpu_custom_call" | custom-call | tf_op jit(solution)/shard_map/pallas_call | solution.py:351
  165.9 0.0 copy-start
  165.9 2.4 %copy.17 = bf16[1,128,4096]{2,1,0:T(8,128)(2,1)} copy(bf16[1,128,4096]{2,1,0:T(8,128)(2,1)} %bitcast.12) | data formatting | bytes 2097152
  168.3 0.0 copy-done
  168.3 1.0 copy.18
Async XLA Ops:
  0.6 0.7 copy-start.1
  2.1 0.7 copy-start.2
  165.9 2.4 %copy-start = (bf16[128,4096]{1,0:T(8,128)(2,1)S(1)}, bf16[128,4096]{1,0:T(8,128)(2,1)}, u32[]{:S(2)}) copy-start(bf16[128,4096]{1,0:T(8,128)(2,1)} %get-tuple-element.5) | copy-start | bytes 3145732

commit v2 on v1

v2 whole, which is shorter than its diff:
```python
import functools
import math

import jax
import jax.numpy as jnp
from jax import lax
from jax.experimental import pallas as pl
from jax.experimental.pallas import tpu as pltpu
from jax.sharding import PartitionSpec as P

QUERY_HEADS = 64
KEY_VALUE_HEADS = 8
GROUP = QUERY_HEADS // KEY_VALUE_HEADS
D = 128
NST = 128
HP = 64
Z_RING = 8
ORDER = (
    ("ring", 0), ("inner", 0, 1), ("ring", 1), ("inner", 1, 2), ("ring", 2), ("queries",), ("attend", 0),
    ("ring", 3), ("attend", 1), ("scan",), ("ring", 4), ("attend", 2), ("finish", 0, 1), ("attend", 3),
    ("finish", 1, 3), ("attend", 4), ("finish", 3, 4),
)
MESH = pl.DeviceIdType.MESH
NEG = -1e30
HIGH = lax.Precision.HIGHEST
F32 = jnp.float32
BF16 = jnp.bfloat16


def nt_dot(a, b):
    return lax.dot_general(a, b, (((1,), (1,)), ((), ())), preferred_element_type=F32)


def section_kernel(
    dims,
    x_hbm, gate_hbm, step_ref, maps_ref, rate_ref, skip_ref, q_hbm, k_hbm, v_hbm, src_ref,
    mo_ref, sq_ref, ao_ref,
    x_ref, gate_ref, srcs, srcb, kv, qb, sb, inbox, so, sin, yb, cum_e, ecum_e, tail_e, skip_e, cum_t, dt_t, gram,
    kt, mx, ls, acc, ob, gb, sqs,
    loc, src_send, src_recv, yk_send, yk_recv, q_send, q_recv, ring_send, ring_recv,
    s_send, s_recv, r_send, r_recv, ao_send, ao_recv, mo_send, mo_recv, sq_send, sq_recv,
):
    nx, ny, nz, T, em = dims
    nc = ny * nz
    seg = lax.axis_index("segment")
    me = lax.axis_index("ctx")
    tp = lax.axis_index("tp")
    y = me // nz
    z = lax.rem(me, nz)
    after = lax.rem(seg + 1, nx)
    before = lax.rem(seg + nx - 1, nx)
    half = nz // 2

    def remote(src, dst, ssem, rsem, dev):
        return pltpu.make_async_remote_copy(
            src_ref=src, dst_ref=dst, send_sem=ssem, recv_sem=rsem, device_id=dev, device_id_type=MESH
        )

    def at_ctx(c):
        return (seg, c, tp)

    load_x = pltpu.make_async_copy(x_hbm, x_ref, loc.at[0])
    load_gate = pltpu.make_async_copy(gate_hbm, gate_ref, loc.at[1])
    load_x.start()
    load_gate.start()

    barrier = pltpu.get_barrier_semaphore()
    for i in range(ny):
        pl.semaphore_signal(barrier, inc=1, device_id=(before, i * nz + z, tp), device_id_type=MESH)

    @pl.loop(1, nc)
    def _(i):
        pl.semaphore_signal(barrier, inc=1, device_id=at_ctx(lax.rem(me + i, nc)), device_id_type=MESH)

    pl.semaphore_signal(barrier, inc=1, device_id=(before, me, 1 - tp), device_id_type=MESH)

    def col(i, w):
        return pl.ds(pl.multiple_of(i * w, w), w)

    heads = em // HP
    row = lax.broadcasted_iota(jnp.int32, (T, T), 0)
    lane = lax.broadcasted_iota(jnp.int32, (T, T), 1)
    low = (row >= lane)
    dt = step_ref[...].astype(F32)
    logs = -rate_ref[...] * dt
    cum = jnp.dot(low.astype(F32), logs, precision=HIGH, preferred_element_type=F32)
    srcs[...] = jnp.full((8, 128), src_ref[0].astype(F32), F32)
    pl.semaphore_wait(barrier, nc - 1 + ny + 1)

    def src_copy():
        return remote(srcs, srcb, src_send, src_recv, (after, me, tp))

    def yk_copy(i, kvi, src):
        o = lax.rem(y + i, ny)
        return remote(
            src.at[:, col(o, D)], kv.at[z, kvi, pl.ds(pl.multiple_of(y * T, T), T)],
            yk_send.at[i, kvi], yk_recv.at[y, kvi], (after, o * nz + z, tp),
        )

    def q_copy(i):
        o = lax.rem(y + i, ny)
        return remote(
            q_hbm.at[:, col(o, GROUP * D)], qb.at[y], q_send.at[i], q_recv.at[y], (after, o * nz + z, tp)
        )

    for i in range(ny):
        yk_copy(i, 0, k_hbm).start()
        yk_copy(i, 1, v_hbm).start()
    src_copy().start()
    for i in range(ny):
        q_copy(i).start()

    def split3(a):
        hi = a.astype(BF16)
        rest = a - hi.astype(F32)
        mid = rest.astype(BF16)
        return [hi, mid, (rest - mid.astype(F32)).astype(BF16)]

    last = cum[T - 1:T, :]
    tail = jnp.exp(last - cum) * dt
    ecum = jnp.exp(cum)
    cum_t[...] = cum.T
    dt_t[...] = dt.T
    width = min(512, em)
    hrow = lax.broadcasted_iota(jnp.int32, (heads, width), 0) * HP
    hcol = lax.broadcasted_iota(jnp.int32, (heads, width), 1)

    def widen(values, put):
        stack = jnp.concatenate(split3(values), axis=1)
        for j in range(em // width):
            off = hcol + j * width - hrow
            pick = ((off >= 0) & (off < HP)).astype(F32).astype(BF16)
            wide = jnp.dot(stack, jnp.concatenate([pick] * 3, axis=0), preferred_element_type=F32)
            put(wide, slice(j * width, (j + 1) * width))

    def put_first(wide, sl):
        tail_e[:, sl] = wide[:T]
        ecum_e[:, sl] = wide[T:]

    def put_second(wide, sl):
        cum_e[:, sl] = wide[:T]
        skip_e[:, sl] = wide[T:T + 8]

    widen(jnp.concatenate([tail, ecum], axis=0), put_first)

    right = at_ctx(y * nz + lax.rem(z + 1, nz))
    left = at_ctx(y * nz + lax.rem(z + nz - 1, nz))

    def ring_copy(b, kvi, way):
        return remote(
            kv.at[b, kvi], kv.at[b, kvi], ring_send.at[way, b, kvi], ring_recv.at[b, kvi],
            right if way == 0 else left,
        )

    reach = [[half, half - 1], [half - 1, half]]

    def ring_step(s):
        for kvi in range(2):
            for way in range(2):
                b = lax.rem(z + nz - s, nz) if way == 0 else lax.rem(z + s, nz)
                if 0 < s <= reach[way][kvi]:
                    ring_copy(b, kvi, way).wait_recv()
                if s < reach[way][kvi]:
                    ring_copy(b, kvi, way).start()

    b_mat = maps_ref[:, :NST]
    c_mat = maps_ref[:, NST:]
    gram[...] = jnp.where(low, nt_dot(c_mat, b_mat), 0.0)
    b_t = b_mat.astype(F32).T.astype(BF16)
    sub16 = lax.broadcasted_iota(jnp.int32, (16, D), 0)

    def state_copy(i, p):
        return remote(sb.at[p], inbox.at[me], s_send.at[i], s_recv.at[me], at_ctx(p))

    def state_of(p):
        scaled = (x_ref[:, col(p, 128)].astype(F32) * tail_e[:, col(p, 128)]).astype(BF16)
        chunk = jnp.dot(b_t, scaled, preferred_element_type=F32)
        decay = ecum_e[T - 1:T, col(p, 128)]
        high = decay.astype(BF16).astype(F32)
        rest = jnp.where(sub16 < 8, high, decay - high)
        return chunk.astype(BF16), rest.astype(BF16)

    load_x.wait()

    @pl.loop(1, nc)
    def _(i):
        p = lax.rem(me + i, nc)
        chunk, rest = state_of(p)
        sb[p, 0:NST] = chunk
        sb[p, NST:NST + 16] = rest
        state_copy(i, p).start()

    chunk, rest = state_of(me)
    inbox[me, 0:NST] = chunk
    inbox[me, NST:NST + 16] = rest

    def wait_yk(c, kvi):
        remote(
            k_hbm.at[:, col(0, D)], kv.at[z, kvi, c * T:(c + 1) * T], yk_send.at[0, kvi], yk_recv.at[c, kvi],
            (after, me, tp),
        ).wait_recv()

    widen(jnp.concatenate([cum, jnp.broadcast_to(skip_ref[...], (16, heads))], axis=0), put_second)
    for c in range(ny):
        wait_yk(c, 0)
        wait_yk(c, 1)

    def inner(p):
        xt = x_ref[:, col(p, 128)]
        ce = cum_e[:, col(p, 128)]
        g = gram[...]
        outs = []
        for k in range(2):
            diff = ce[:, k * HP:k * HP + 1] - cum_t[pl.ds(2 * p + k, 1), :]
            w = g * jnp.exp(jnp.minimum(diff, 0.0)) * dt_t[pl.ds(2 * p + k, 1), :]
            outs.append(jnp.dot(w.astype(BF16), xt, preferred_element_type=F32))
        mixed = jnp.where(lane < HP, outs[0], outs[1])
        yb[:, col(p, 128)] = mixed + skip_e[0:1, col(p, 128)] * xt.astype(F32)

    def back_copy(c):
        return remote(so.at[c], sin.at[me], r_send.at[c], r_recv.at[me], at_ctx(c))

    def scan_step(c, carry):
        @pl.when(c != me)
        def _():
            remote(sb.at[0], inbox.at[c], s_send.at[0], s_recv.at[c], at_ctx(c)).wait_recv()
        so[c] = carry.astype(BF16)
        rest = inbox[c, NST:NST + 16].astype(F32)
        return carry * (rest[0:1] + rest[8:9]) + inbox[c, 0:NST].astype(F32)

    def scan():
        lax.fori_loop(0, nc, scan_step, jnp.zeros((NST, 128), F32))

        @pl.loop(1, nc)
        def _(i):
            back_copy(lax.rem(me + i, nc)).start()
        sin[me] = so[me]

    scale2 = 1.0 / math.sqrt(D) * math.log2(math.e)
    R = GROUP * T
    lane_t = lax.broadcasted_iota(jnp.int32, (1, T), 1)

    def attend_start():
        remote(srcs, srcb, src_send, src_recv, (after, me, tp)).wait_recv()
        for c in range(ny):
            remote(q_hbm.at[:, col(0, GROUP * D)], qb.at[c], q_send.at[0], q_recv.at[c], (after, me, tp)).wait_recv()
        mx[...] = jnp.full((ny, R, T), NEG, F32)
        ls[...] = jnp.zeros((ny, R, T), F32)
        acc[...] = jnp.zeros((ny, R, D), F32)

    def attend(blocks, final):
        n = len(blocks)
        keys = ny * T
        for i, b in enumerate(blocks):
            kt[:, i * keys:(i + 1) * keys] = kv[b, 0].T

        @pl.loop(0, ny)
        def _(c):
            pos = (row + (c * (nz * T) + z * T + 1)).astype(F32)
            lim = jnp.maximum(pos, srcb[0:1, :])
            lim = jnp.concatenate([lim] * GROUP, axis=0)
            q = jnp.concatenate([qb[c, :, g * D:(g + 1) * D] for g in range(GROUP)], axis=0)
            s = jnp.dot(q, kt[:, 0:n * keys], preferred_element_type=F32)
            parts = []
            top = None
            for i, b in enumerate(blocks):
                for j in range(ny):
                    part = s[:, i * keys + j * T:i * keys + (j + 1) * T]
                    if j > 0:
                        kpos = (lane_t + (j * (nz * T) + b * T)).astype(F32)
                        part = jnp.where(kpos < lim, part, NEG)
                    parts.append(part)
                    top = part if top is None else jnp.maximum(top, part)
            m_old = mx[c]
            m = jnp.maximum(m_old, jnp.max(top, axis=-1, keepdims=True))
            a = jnp.exp2((m_old - m) * scale2)
            mx[c] = m
            ws = [jnp.exp2((part - m) * scale2) for part in parts]
            total = ls[c] * a
            for w in ws:
                total = total + w
            w_all = jnp.concatenate([w.astype(BF16) for w in ws], axis=1)
            v_all = jnp.concatenate([kv[b, 1] for b in blocks], axis=0)
            o = acc[c] * a + jnp.dot(w_all, v_all, preferred_element_type=F32)
            if final:
                o = (o / jnp.sum(total, axis=-1, keepdims=True)).astype(BF16)
                for g in range(GROUP):
                    ob[c, :, g * D:(g + 1) * D] = o[g * T:(g + 1) * T]

                @pl.when(c != y)
                def _():
                    out_copy(c).start()

                @pl.when(c == y)
                def _():
                    own_out().start()
            else:
                ls[c] = total
                acc[c] = o

    def out_copy(c):
        return remote(ob.at[c], ao_ref.at[:, col(y, GROUP * D)], ao_send.at[c], ao_recv.at[y], at_ctx(c * nz + z))

    def own_out():
        return pltpu.make_async_copy(ob.at[y], ao_ref.at[:, col(y, GROUP * D)], loc.at[2])

    def sq_copy(other):
        return remote(
            sqs, sq_ref.at[tp], sq_send.at[other], sq_recv.at[tp], (after, me, lax.rem(tp + other, 2))
        )

    def gated_copy(p):
        return remote(
            gb.at[p], mo_ref.at[:, col(p, 128)], mo_send.at[p], mo_recv.at[p], (after, me, tp)
        )

    def finish_step(i):
        p = lax.rem(me + nc - i, nc)

        @pl.when(i > 0)
        def _():
            remote(so.at[0], sin.at[p], r_send.at[0], r_recv.at[p], at_ctx(p)).wait_recv()
        entered = jnp.dot(c_mat, sin[p], preferred_element_type=F32)
        raw = (yb[:, col(p, 128)] + ecum_e[:, col(p, 128)] * entered).astype(BF16).astype(F32)
        g = gate_ref[:, col(p, 128)].astype(F32)
        gated = raw * (g / (1.0 + jnp.exp(-g)))
        gb[p] = gated.astype(BF16)
        gated_copy(p).start()
        sqs[...] += gated * gated

    sqs[...] = jnp.zeros((T, 128), F32)
    load_gate.wait()

    def near(s):
        if s == 0 or s == half:
            return [lax.rem(z + s, nz)]
        return [lax.rem(z + nz - s, nz), lax.rem(z + s, nz)]

    quarter = nc // 4
    for item in ORDER:
        if item[0] == "ring":
            ring_step(item[1])
        elif item[0] == "inner":
            @pl.loop(item[1] * nc // 2, item[2] * nc // 2)
            def _(p):
                inner(p)
        elif item[0] == "queries":
            attend_start()
        elif item[0] == "attend":
            attend(near(item[1]), item[1] == half)
        elif item[0] == "scan":
            scan()
        else:
            @pl.loop(item[1] * quarter, item[2] * quarter)
            def _(i):
                finish_step(i)
            if item[2] == 4:
                for other in range(2):
                    sq_copy(other).start()

    for i in range(ny):
        yk_copy(i, 0, k_hbm).wait_send()
        yk_copy(i, 1, v_hbm).wait_send()
        q_copy(i).wait_send()
    src_copy().wait_send()
    for s in range(half):
        for kvi in range(2):
            for way in range(2):
                b = lax.rem(z + nz - s, nz) if way == 0 else lax.rem(z + s, nz)
                if s < reach[way][kvi]:
                    ring_copy(b, kvi, way).wait_send()

    @pl.loop(1, nc)
    def _(i):
        p = lax.rem(me + i, nc)
        state_copy(i, p).wait_send()
        back_copy(p).wait_send()

    own_out().wait()
    for i in range(1, ny):
        c = lax.rem(y + i, ny)
        out_copy(c).wait_send()
        remote(ob.at[0], ao_ref.at[:, col(c, GROUP * D)], ao_send.at[0], ao_recv.at[c], at_ctx(me)).wait_recv()

    @pl.loop(0, nc)
    def _(p):
        gated_copy(p).wait_send()
        gated_copy(p).wait_recv()
    for k in range(2):
        sq_copy(k).wait_send()
        remote(sqs, sq_ref.at[k], sq_send.at[k], sq_recv.at[k], (after, me, tp)).wait_recv()


def on_device(mamba_input, mamba_gate, step_size, state_maps, decay_rate, skip_gain, norm_gain,
              queries, keys, values, source_len, *, dims):
    nx, ny, nz, T, em = dims
    nc = ny * nz
    vmem = pl.BlockSpec(memory_space=pltpu.VMEM)
    hbm = pl.BlockSpec(memory_space=pl.ANY)
    R = GROUP * T
    DMA = pltpu.SemaphoreType.DMA
    out = jax.ShapeDtypeStruct((T, em), BF16)
    gated, squares, ao = pl.pallas_call(
        functools.partial(section_kernel, dims),
        out_shape=(
            out, jax.ShapeDtypeStruct((2, T, 128), F32), jax.ShapeDtypeStruct((T, ny * GROUP * D), BF16)
        ),
        in_specs=[hbm, hbm, vmem, vmem, vmem, vmem, hbm, hbm, hbm, pl.BlockSpec(memory_space=pltpu.SMEM)],
        out_specs=(hbm, hbm, hbm),
        scratch_shapes=[
            pltpu.VMEM((T, em), BF16),
            pltpu.VMEM((T, em), BF16),
            pltpu.VMEM((8, 128), F32),
            pltpu.VMEM((8, 128), F32),
            pltpu.VMEM((nz, 2, ny * T, D), BF16),
            pltpu.VMEM((ny, T, GROUP * D), BF16),
            pltpu.VMEM((nc, NST + 16, 128), BF16),
            pltpu.VMEM((nc, NST + 16, 128), BF16),
            pltpu.VMEM((nc, NST, 128), BF16),
            pltpu.VMEM((nc, NST, 128), BF16),
            pltpu.VMEM((T, em), F32),
            pltpu.VMEM((T, em), F32),
            pltpu.VMEM((T, em), F32),
            pltpu.VMEM((T, em), F32),
            pltpu.VMEM((8, em), F32),
            pltpu.VMEM((em // HP, T), F32),
            pltpu.VMEM((em // HP, T), F32),
            pltpu.VMEM((T, T), F32),
            pltpu.VMEM((D, 2 * ny * T), BF16),
            pltpu.VMEM((ny, R, T), F32),
            pltpu.VMEM((ny, R, T), F32),
            pltpu.VMEM((ny, R, D), F32),
            pltpu.VMEM((ny, T, GROUP * D), BF16),
            pltpu.VMEM((nc, T, 128), BF16),
            pltpu.VMEM((T, 128), F32),
            DMA((3,)), DMA(()), DMA(()),
            DMA((ny, 2)), DMA((ny, 2)), DMA((ny,)), DMA((ny,)),
            DMA((2, nz, 2)), DMA((nz, 2)), DMA((nc,)), DMA((nc,)), DMA((nc,)), DMA((nc,)),
            DMA((ny,)), DMA((ny,)), DMA((nc,)), DMA((nc,)), DMA((2,)), DMA((2,)),
        ],
        compiler_params=pltpu.CompilerParams(
            collective_id=0, has_side_effects=True, vmem_limit_bytes=56 << 20
        ),
    )(
        mamba_input[0], mamba_gate[0], step_size[0], state_maps[0],
        decay_rate[None, :], skip_gain[None, :],
        queries[0], keys[0], values[0], source_len,
    )
    total = jnp.sum(squares, axis=(0, 2))
    factor = lax.rsqrt(total / (2 * em) + 1e-5)[:, None]
    mo = (gated.astype(F32) * factor * norm_gain[None, :]).astype(BF16)
    return mo[None], ao[None]


def solution(mesh):
    nx, nc = mesh.shape["segment"], mesh.shape["ctx"]
    nz = min(Z_RING, nc)
    placed = (
        P("segment", "ctx", "tp"), P("segment", "ctx", "tp"), P("segment", "ctx", "tp"),
        P("segment", "ctx", None), P("tp"), P("tp"), P("tp"),
        P("segment", "ctx", "tp"), P("segment", "ctx", "tp"), P("segment", "ctx", "tp"), P("segment"),
    )
    dims = (nx, nc // nz, nz, 128, 128 * nc)
    return jax.shard_map(
        functools.partial(on_device, dims=dims),
        mesh=mesh,
        in_specs=placed,
        out_specs=(P("segment", "ctx", "tp"), P("segment", "ctx", "tp")),
        check_vma=False,
    )
```

time: 169 us -> 115 us (0.68)
  the two profiles are of different devices: /device:TPU:121 before, /device:TPU:1 now
where the time goes in v2:
time: 115 us; the launch traced here: 114 us
  Pallas kernels  107 us (93%)
  other arithmetic  3.62 us (3%)
  local copies, waits for them, and re-layouts  2.41 us (2%)
  between operations  1.32 us (1%)
    pallas_call x1, Pallas kernels, on_device(): pl.pallas_call(functools.partial(section_kernel, dims), out_shape=(out, j...  107 us
    broadcast_in_dim x1, other arithmetic, on_device(): return (mo[None], ao[None])  2.61 us
    unnamed x6, local copies, waits for them, and re-layouts  2.41 us

profile of v2, /device:TPU:1, one launch (start us, length us, event | category | flops | bytes accessed | tf_op | source)
XLA Modules:
  0.0 114.4 jit_solution(9909556369902761412)
XLA Ops:
  1.3 1.4 %copy.13 = bf16[1,128,64]{2,1,0:T(8,128)(2,1)} copy(bf16[1,128,64]{1,2,0:T(8,128)(2,1)} %param.13) | data formatting | bytes 32768 | tf_op args[2]
  2.7 0.0 copy-start.1
  2.7 107.1 %shard_map.122 = (bf16[128,4096]{1,0:T(8,128)(2,1)}, f32[2,128,128]{2,1,0:T(8,128)}, bf16[128,4096]{1,0:T(8,128)(2,1)}) custom-call(bf16[128,4096]{1,0:T(8,128)(2,1)} %bitcast.13, bf16[128,4096]{1,0:T(8,128)(2,1)} %bitcast.14, bf16[128,64]{1,0:T(8,128)(2,1)} %bitcast.16, bf16[128,256]{1,0:T(8,128)(2,1)} %bitcast.19, f32[1,64]{1,0:T(1,128)} %bitcast.20, ...), custom_call_target="tpu_custom_call" | custom-call | tf_op jit(solution)/shard_map/pallas_call | solution.py:403
  109.8 1.0 reduce_sum.9
  110.8 0.0 copy-done.1
  110.9 0.0 copy-start
  110.9 2.6 %fusion = bf16[1,128,4096]{2,1,0:T(8,128)(2,1)} fusion(bf16[128,4096]{1,0:T(8,128)(2,1)} %get-tuple-element.5, f32[4096]{0:T(1024)S(1)} %copy-done.1, f32[128]{0:T(128)S(1)} %add_rsqrt_fusion), kind=kLoop, calls=%fused_computation.1 | loop fusion | flops 2097152 | bytes 2114048 | tf_op jit(solution)/shard_map/broadcast_in_dim | solution.py:452
  113.5 0.0 copy-done
  113.5 1.0 copy.16
  (1 shorter events, 0.0 us)
Async XLA Ops:
  2.7 108.1 %copy-start.1 = (f32[4096]{0:T(1024)S(1)}, f32[4096]{0:T(1024)}, u32[]{:S(2)}) copy-start(f32[4096]{0:T(1024)} %param.17) | copy-start | bytes 49156
  110.9 2.6 %copy-start = (bf16[128,4096]{1,0:T(8,128)(2,1)S(1)}, bf16[128,4096]{1,0:T(8,128)(2,1)}, u32[]{:S(2)}) copy-start(bf16[128,4096]{1,0:T(8,128)(2,1)} %get-tuple-element.7) | copy-start | bytes 3145732

commit v3 on v2

--- a/solution.py
+++ b/solution.py
@@ -15,10 +15,11 @@
 NST = 128
 HP = 64
 Z_RING = 8
+STRIDE = 13
 ORDER = (
-    ("ring", 0), ("inner", 0, 1), ("ring", 1), ("inner", 1, 2), ("ring", 2), ("queries",), ("attend", 0),
-    ("ring", 3), ("attend", 1), ("scan",), ("ring", 4), ("attend", 2), ("finish", 0, 1), ("attend", 3),
-    ("finish", 1, 3), ("attend", 4), ("finish", 3, 4),
+    ("ring", 0), ("inner", 0, 1), ("ring", 1), ("inner", 1, 2), ("ring", 2), ("queries",),
+    ("attend", 0), ("ring", 3), ("scan",), ("attend", 1), ("attend", 2), ("finish", 0, 1),
+    ("attend", 3), ("finish", 1, 3), ("ring", 4), ("attend", 4), ("finish", 3, 4),
 )
 MESH = pl.DeviceIdType.MESH
 NEG = -1e30
@@ -107,8 +108,6 @@
         yk_copy(i, 0, k_hbm).start()
         yk_copy(i, 1, v_hbm).start()
     src_copy().start()
-    for i in range(ny):
-        q_copy(i).start()
 
     def split3(a):
         hi = a.astype(BF16)
@@ -184,11 +183,17 @@
 
     @pl.loop(1, nc)
     def _(i):
-        p = lax.rem(me + i, nc)
+        p = lax.rem(me + i * STRIDE, nc)
         chunk, rest = state_of(p)
         sb[p, 0:NST] = chunk
         sb[p, NST:NST + 16] = rest
         state_copy(i, p).start()
+
+        @pl.when(lax.rem(i, nc // ny) == 0)
+        def _():
+            q_copy(i // (nc // ny) - 1).start()
+
+    q_copy(ny - 1).start()
 
     chunk, rest = state_of(me)
     inbox[me, 0:NST] = chunk
@@ -233,7 +238,7 @@
 
         @pl.loop(1, nc)
         def _(i):
-            back_copy(lax.rem(me + i, nc)).start()
+            back_copy(lax.rem(me + i * STRIDE, nc)).start()
         sin[me] = so[me]
 
     scale2 = 1.0 / math.sqrt(D) * math.log2(math.e)
@@ -315,7 +320,7 @@
         )
 
     def finish_step(i):
-        p = lax.rem(me + nc - i, nc)
+        p = lax.rem(me + (nc - i) * STRIDE, nc)
 
         @pl.when(i > 0)
         def _():
@@ -355,6 +360,7 @@
             def _(i):
                 finish_step(i)
             if item[2] == 4:
+                sqs[...] = jnp.broadcast_to(jnp.sum(sqs[...], axis=-1, keepdims=True), (T, 128))
                 for other in range(2):
                     sq_copy(other).start()
 
@@ -446,8 +452,7 @@
         decay_rate[None, :], skip_gain[None, :],
         queries[0], keys[0], values[0], source_len,
     )
-    total = jnp.sum(squares, axis=(0, 2))
-    factor = lax.rsqrt(total / (2 * em) + 1e-5)[:, None]
+    factor = lax.rsqrt((squares[0, :, :1] + squares[1, :, :1]) / (2 * em) + 1e-5)
     mo = (gated.astype(F32) * factor * norm_gain[None, :]).astype(BF16)
     return mo[None], ao[None]
 

time: 115 us -> 113 us (0.983)
    pallas_call x1, Pallas kernels: 107 us -> 106 us  [on_device(): pl.pallas_call(functools.partial(section_kernel, dims), out_shape=(out, j...]
where the time goes in v3:
time: 113 us
  Pallas kernels  106 us (94%)
  other arithmetic  3.59 us (3%)
  local copies, waits for them, and re-layouts  2.41 us (2%)
  between operations  1.31 us (1%)
    pallas_call x1, Pallas kernels, on_device(): pl.pallas_call(functools.partial(section_kernel, dims), out_shape=(out, j...  106 us
    broadcast_in_dim x1, other arithmetic, on_device(): return (mo[None], ao[None])  2.61 us
    unnamed x6, local copies, waits for them, and re-layouts  2.41 us

profile of v3, /device:TPU:1, one launch (start us, length us, event | category | flops | bytes accessed | tf_op | source)
XLA Modules:
  0.0 113.0 jit_solution(10046588230532326029)
XLA Ops:
  1.3 1.4 %copy.14 = bf16[1,128,64]{2,1,0:T(8,128)(2,1)} copy(bf16[1,128,64]{1,2,0:T(8,128)(2,1)} %param.13) | data formatting | bytes 32768 | tf_op args[2]
  2.7 0.0 copy-start.1
  2.7 105.7 %shard_map.122 = (bf16[128,4096]{1,0:T(8,128)(2,1)}, f32[2,128,128]{2,1,0:T(8,128)}, bf16[128,4096]{1,0:T(8,128)(2,1)}) custom-call(bf16[128,4096]{1,0:T(8,128)(2,1)} %bitcast.13, bf16[128,4096]{1,0:T(8,128)(2,1)} %bitcast.14, bf16[128,64]{1,0:T(8,128)(2,1)} %bitcast.16, bf16[128,256]{1,0:T(8,128)(2,1)} %bitcast.19, f32[1,64]{1,0:T(1,128)} %bitcast.20, ...), custom_call_target="tpu_custom_call" | custom-call | tf_op jit(solution)/shard_map/pallas_call | solution.py:409
  108.4 1.0 rsqrt_reduce_fusion
  109.4 0.0 copy-done.1
  109.4 0.0 copy-start
  109.4 2.6 %fusion = bf16[1,128,4096]{2,1,0:T(8,128)(2,1)} fusion(bf16[128,4096]{1,0:T(8,128)(2,1)} %get-tuple-element.5, f32[4096]{0:T(1024)S(1)} %copy-done.1, f32[128]{0:T(128)S(1)} %rsqrt_reduce_fusion), kind=kLoop, calls=%fused_computation.1 | loop fusion | flops 2097152 | bytes 2114048 | tf_op jit(solution)/shard_map/broadcast_in_dim | solution.py:457
  112.0 0.0 copy-done
  112.0 1.0 copy.17
Async XLA Ops:
  2.7 106.7 %copy-start.1 = (f32[4096]{0:T(1024)S(1)}, f32[4096]{0:T(1024)}, u32[]{:S(2)}) copy-start(f32[4096]{0:T(1024)} %param.17) | copy-start | bytes 49156
  109.4 2.6 %copy-start = (bf16[128,4096]{1,0:T(8,128)(2,1)S(1)}, bf16[128,4096]{1,0:T(8,128)(2,1)}, u32[]{:S(2)}) copy-start(bf16[128,4096]{1,0:T(8,128)(2,1)} %get-tuple-element.7) | copy-start | bytes 3145732
